TPU v7x, 256 devices: a whole 4x4x8 slice. The times are simulated.
256 devices in a mesh: expert: 64 (over y, z_hi, x, core), hidden: 4 (over z_lo).
Axes of the slice: x: 4, y: 4, z: 8 (z_hi: 2, z_lo: 4; z = z_hi * 4 + z_lo), core: 2. Of those that a mesh axis runs over, the one named last changes fastest.
Arguments:
- tokens: bfloat16 [50176, 768], P(('expert', 'hidden')), may hold values from -512 to 512
- out_grad: bfloat16 [50176, 768], P(('expert', 'hidden')), may hold values from -12 to 12
- slot_router: bfloat16 [768, 256], replicated, may hold values from -0.5 to 0.5
- weight_in: bfloat16 [128, 768, 3072], P('expert', None, 'hidden'), may hold values from -0.21875 to 0.21875
- weight_out: bfloat16 [128, 3072, 768], P('expert', 'hidden'), may hold values from -0.109375 to 0.109375
Outputs:
- token_grad: bfloat16 [50176, 768], P(('expert', 'hidden'))
- router_grad: float32 [768, 256], P('hidden', 'expert')
- weight_in_grad: bfloat16 [128, 768, 3072], P('expert', None, 'hidden')
- weight_out_grad: bfloat16 [128, 3072, 768], P('expert', 'hidden')
All inputs are finite; a program needn't handle non-finite values.
Results may differ from a plain program's by a relative error of at most 0.019.
Values may be sent and summed in bfloat16 or wider, within the bound.
A program may use at most 64 MiB of HBM per device.

v0:
```python
import jax
import jax.numpy as jnp
from jax import lax
from jax.sharding import PartitionSpec as P

D = 768
SLOTS = 2
TOK = 196


def gelu_value(values):
    return 0.5 * values * (1.0 + lax.erf(values * 0.7071067811865476))


def gelu_slope(values):
    return (
        0.5 * (1.0 + lax.erf(values * 0.7071067811865476))
        + values * jnp.exp(-0.5 * values * values) * 0.3989422804014327
    )


def to_experts(stacked_slots):
    crossed = lax.all_to_all(stacked_slots, "expert", split_axis=2, concat_axis=0, tiled=True)
    arrived = lax.all_gather(crossed, "hidden", axis=0, tiled=True)
    return arrived


def to_owners(partials):
    rounded = lax.optimization_barrier(partials.astype(jnp.bfloat16))
    summed = lax.psum_scatter(
        rounded.astype(jnp.float32).astype(jnp.bfloat16), "hidden", scatter_dimension=0, tiled=True
    )
    result = lax.all_to_all(summed, "expert", split_axis=0, concat_axis=2, tiled=True)
    return result


def per_device(tokens, out_grad, slot_router, weight_in, weight_out):
    images = tokens.shape[0] // TOK
    local_experts = weight_in.shape[0]
    inputs = tokens.reshape(images, TOK, D)
    out_grads = out_grad.reshape(images, TOK, D)
    logits = jnp.einsum("btd,dc->btc", inputs, slot_router, preferred_element_type=jnp.float32)
    dispatch = jax.nn.softmax(logits, axis=1)
    combine = jax.nn.softmax(logits, axis=2)
    dispatch16 = dispatch.astype(jnp.bfloat16)
    combine16 = combine.astype(jnp.bfloat16)
    slot_in = jnp.einsum(
        "btc,btd->bcd", dispatch16, inputs, preferred_element_type=jnp.float32
    ).astype(jnp.bfloat16)
    slot_grad = jnp.einsum(
        "btc,btd->bcd", combine16, out_grads, preferred_element_type=jnp.float32
    ).astype(jnp.bfloat16)
    arrived = to_experts(slot_in[:, None])
    received = arrived[:, 0]
    row_count = received.shape[0]
    slot_inputs = received.reshape(row_count, local_experts, SLOTS, D)
    pre_act = jnp.einsum(
        "resd,edf->resf", slot_inputs, weight_in, preferred_element_type=jnp.float32
    )
    activated = gelu_value(pre_act).astype(jnp.bfloat16)
    partial_value = jnp.einsum(
        "resf,efd->resd", activated, weight_out, preferred_element_type=jnp.float32
    )
    slot_inputs, pre_act, activated, forward_part = (
        slot_inputs,
        pre_act,
        activated,
        partial_value.reshape(row_count, 1, local_experts * SLOTS, D),
    )
    slot_out = to_owners(forward_part)[:, 0]
    arrived_grad = to_experts(slot_grad[:, None])
    received_grad = arrived_grad[:, 0]
    row_count = received_grad.shape[0]
    slot_grads = received_grad.reshape(row_count, local_experts, SLOTS, D)
    d_act = jnp.einsum("resd,efd->resf", slot_grads, weight_out, preferred_element_type=jnp.float32)
    d_pre = (d_act * gelu_slope(pre_act)).astype(jnp.bfloat16)
    grad_second = jnp.einsum(
        "resf,resd->efd", activated, slot_grads, preferred_element_type=jnp.float32
    ).astype(jnp.bfloat16)
    grad_first = jnp.einsum(
        "resd,resf->edf", slot_inputs, d_pre, preferred_element_type=jnp.float32
    ).astype(jnp.bfloat16)
    partial_value = jnp.einsum(
        "resf,edf->resd", d_pre, weight_in, preferred_element_type=jnp.float32
    )
    backward_part = partial_value.reshape(row_count, 1, local_experts * SLOTS, D)
    slot_in_grad = to_owners(backward_part)[:, 0]
    d_combine = jnp.einsum("btd,bcd->btc", out_grads, slot_out, preferred_element_type=jnp.float32)
    d_dispatch = jnp.einsum(
        "btd,bcd->btc", inputs, slot_in_grad, preferred_element_type=jnp.float32
    )
    from_combine = combine * (d_combine - jnp.sum(combine * d_combine, axis=2, keepdims=True))
    from_dispatch = dispatch * (d_dispatch - jnp.sum(dispatch * d_dispatch, axis=1, keepdims=True))
    d_logits = (from_combine + from_dispatch).astype(jnp.bfloat16)
    token_grad = (
        jnp.einsum("btc,bcd->btd", dispatch16, slot_in_grad, preferred_element_type=jnp.float32)
        + jnp.einsum("btc,dc->btd", d_logits, slot_router, preferred_element_type=jnp.float32)
    ).astype(jnp.bfloat16)
    router_term = jnp.einsum("btd,btc->dc", inputs, d_logits, preferred_element_type=jnp.float32)
    router_sum = lax.psum(router_term, ("expert", "hidden"))
    row_count = router_term.shape[0] // lax.axis_size("hidden")
    col_count = router_term.shape[1] // lax.axis_size("expert")
    router_grad = lax.dynamic_slice(
        router_sum,
        (lax.axis_index("hidden") * row_count, lax.axis_index("expert") * col_count),
        (row_count, col_count),
    )
    return (token_grad.reshape(images * TOK, D), router_grad, grad_first, grad_second)


def solution(mesh):
    return jax.shard_map(
        per_device,
        mesh=mesh,
        in_specs=(
            P(("expert", "hidden"), None),
            P(("expert", "hidden"), None),
            P(),
            P("expert", None, "hidden"),
            P("expert", "hidden", None),
        ),
        out_specs=(
            P(("expert", "hidden"), None),
            P("hidden", "expert"),
            P("expert", None, "hidden"),
            P("expert", "hidden", None),
        ),
        check_vma=False,
    )
```

profile of v0, /device:TPU:2, one launch (start us, length us, event | category | flops | bytes accessed | tf_op | source)
XLA Modules:
  0.0 541.8 jit_solution(13264223133541740712)
XLA Ops:
  11.4 3.9 reduce.16
  16.5 28.7 %all_to_all.42 = bf16[64,2,1536]{2,1,0:T(2,128)(2,1)} all-to-all(bf16[64,2,1536]{2,1,0:T(2,128)(2,1)S(1)} %reshape.157), channel_id=1, replica_groups=mesh['expert'=64,'hidden'=4] {'expert'}, dimensions={0} | all-to-all | bytes 786432 | tf_op jit(solution)/shard_map/all_to_all | solution.py:23
  45.3 2.7 reshape.158
  48.0 3.0 bitcast_reduce_fusion.1
  55.1 3.9 reduce.17
  60.2 26.7 %all_to_all.43 = bf16[64,2,1536]{2,1,0:T(2,128)(2,1)} all-to-all(bf16[64,2,1536]{2,1,0:T(2,128)(2,1)S(1)} %reshape.159), channel_id=1, replica_groups=mesh['expert'=64,'hidden'=4] {'expert'}, dimensions={0} | all-to-all | bytes 786432 | tf_op jit(solution)/shard_map/all_to_all | solution.py:23
  86.9 2.7 reshape.160
  89.7 3.0 bitcast_reduce_fusion
  94.8 7.2 %all-gather.5.cloned.1.call-done = bf16[256,1,4,768]{3,2,1,0:T(4,128)(2,1)} async-done(((bf16[64,1,4,768]{3,2,1,0:T(4,128)(2,1)}), bf16[256,1,4,768]{3,2,1,0:T(4,128)(2,1)}) %all-gather.5.cloned.1.call-update) | async-done | bytes 1572880 | tf_op jit(solution)/shard_map/all_gather | solution.py:24
  104.8 3.0 fusion.9
  107.8 37.1 %all-gather.3.cloned.1.call-done = bf16[256,1,4,768]{3,2,1,0:T(4,128)(2,1)} async-done(((bf16[64,1,4,768]{3,2,1,0:T(4,128)(2,1)}), bf16[256,1,4,768]{3,2,1,0:T(4,128)(2,1)}) %all-gather.3.cloned.1.call-update) | async-done | bytes 1572880 | tf_op jit(solution)/shard_map/all_gather | solution.py:24
  147.1 3.8 fusion.5
  155.0 3.5 fusion.18
  161.2 33.9 %reduce-scatter.9.cloned.1.call-done = bf16[64,3072]{1,0:T(8,128)(2,1)} async-done(((bf16[256,3072]{1,0:T(8,128)(2,1)}), bf16[64,3072]{1,0:T(8,128)(2,1)}) %reduce-scatter.9.cloned.1.call-update) | async-done | bytes 393232
  195.1 2.0 reshape.152
  197.1 10.9 %all-to-all-start.2 = ((bf16[64,1,4,768]{3,2,1,0:T(4,128)(2,1)}), bf16[64,1,4,768]{3,2,1,0:T(4,128)(2,1)S(1)}, u32[]{:S(2)}, u32[]{:S(2)}) async-start(bf16[64,1,4,768]{3,2,1,0:T(4,128)(2,1)} %reshape.152), calls=%async_computation.2 | async-start | bytes 786432 | tf_op jit(solution)/shard_map/all_to_all | solution.py:33
  208.0 37.7 %reduce-scatter.11.cloned.1.call-done = bf16[64,3072]{1,0:T(8,128)(2,1)} async-done(((bf16[256,3072]{1,0:T(8,128)(2,1)}), bf16[64,3072]{1,0:T(8,128)(2,1)}) %reduce-scatter.11.cloned.1.call-update) | async-done | bytes 393232
  245.7 2.0 reshape.154
  247.7 11.1 %all-to-all-start.3 = ((bf16[64,1,4,768]{3,2,1,0:T(4,128)(2,1)}), bf16[64,1,4,768]{3,2,1,0:T(4,128)(2,1)}, u32[]{:S(2)}, u32[]{:S(2)}) async-start(bf16[64,1,4,768]{3,2,1,0:T(4,128)(2,1)} %reshape.154), calls=%async_computation.3 | async-start | bytes 786432 | tf_op jit(solution)/shard_map/all_to_all | solution.py:33
  259.2 4.9 bitcast_convert_fusion
  264.1 2.9 bitcast_convert_fusion.1
  268.4 6.4 %all-to-all-done.3 = bf16[64,1,4,768]{3,2,1,0:T(4,128)(2,1)} async-done(((bf16[64,1,4,768]{3,2,1,0:T(4,128)(2,1)}), bf16[64,1,4,768]{3,2,1,0:T(4,128)(2,1)}, u32[]{:S(2)}, u32[]{:S(2)}) %all-to-all-start.3) | async-done | bytes 393248 | tf_op jit(solution)/shard_map/all_to_all | solution.py:33
  280.7 2.0 fusion.26
  282.7 251.2 %all-reduce.2.cloned.1.call-done = f32[768,256]{0,1:T(8,128)} async-done(((f32[768,256]{0,1:T(8,128)}), f32[768,256]{0,1:T(8,128)}) %all-reduce.2.cloned.1.call-update) | async-done | bytes 786448 | tf_op jit(solution)/shard_map/psum | solution.py:100
  (57 shorter events, 33.5 us)
Async XLA Ops:
  7.2 97.6 %copy-start = (bf16[2,768,768]{2,1,0:T(8,128)(2,1)S(1)}, bf16[2,768,768]{2,1,0:T(8,128)(2,1)}, u32[]{:S(2)}) copy-start(bf16[2,768,768]{2,1,0:T(8,128)(2,1)} %param.8) | copy-start | bytes 7077892
  7.2 94.8 %all-gather.5.cloned.1.call-start = ((), (), s32[]{:S(2)}) async-start(), calls=%async_computation.7 | async-start | bytes 1966080 | tf_op jit(solution)/shard_map/all_gather | solution.py:24
  52.9 92.0 %all-gather.3.cloned.1.call-start = ((), (), s32[]{:S(2)}) async-start(), calls=%async_computation.6 | async-start | bytes 1966080 | tf_op jit(solution)/shard_map/all_gather | solution.py:24
  94.6 100.5 %reduce-scatter.9.cloned.1.call-start = ((), (), s32[]{:S(2)}) async-start(), calls=%async_computation.9 | async-start | bytes 1966080
  103.6 1.1 copy-start.2
  144.9 2.1 copy-start.7
  146.7 4.1 copy-start.4
  150.8 1.4 copy-start.8
  154.9 90.8 %reduce-scatter.11.cloned.1.call-start = ((), (), s32[]{:S(2)}) async-start(), calls=%async_computation.10 | async-start | bytes 1966080
  197.1 50.6 %all-to-all-start.2 = ((bf16[64,1,4,768]{3,2,1,0:T(4,128)(2,1)}), bf16[64,1,4,768]{3,2,1,0:T(4,128)(2,1)S(1)}, u32[]{:S(2)}, u32[]{:S(2)}) async-start(bf16[64,1,4,768]{3,2,1,0:T(4,128)(2,1)} %reshape.152), calls=%async_computation.2 | async-start | bytes 786432 | tf_op jit(solution)/shard_map/all_to_all | solution.py:33
  247.7 16.3 %copy-start.5 = (bf16[64,1,4,768]{3,2,1,0:T(4,128)(2,1)}, bf16[64,1,4,768]{3,2,1,0:T(4,128)(2,1)S(1)}, u32[]{:S(2)}) copy-start(bf16[64,1,4,768]{3,2,1,0:T(4,128)(2,1)S(1)} %all-to-all-done.2) | copy-start | bytes 1179652
  247.7 27.0 %all-to-all-start.3 = ((bf16[64,1,4,768]{3,2,1,0:T(4,128)(2,1)}), bf16[64,1,4,768]{3,2,1,0:T(4,128)(2,1)}, u32[]{:S(2)}, u32[]{:S(2)}) async-start(bf16[64,1,4,768]{3,2,1,0:T(4,128)(2,1)} %reshape.154), calls=%async_computation.3 | async-start | bytes 786432 | tf_op jit(solution)/shard_map/all_to_all | solution.py:33
  258.9 275.0 %all-reduce.2.cloned.1.call-start = ((), (), s32[]{:S(2)}) async-start(), calls=%async_computation.8 | async-start | bytes 1572864 | tf_op jit(solution)/shard_map/psum | solution.py:100
  259.2 4.9 copy-start.3
  259.2 4.9 copy-start.9
  264.1 4.0 copy-start.1
  268.4 9.7 %copy-start.6 = (f32[196,256]{1,0:T(8,128)}, f32[196,256]{1,0:T(8,128)S(1)}, u32[]{:S(2)}) copy-start(f32[196,256]{1,0:T(8,128)S(1)} %convolution_bitcast_fusion.1) | copy-start | bytes 602116
Sparse Core Ops, SparseCore 0:
  53.0 48.9 all-gather.4
  103.8 41.0 all-gather.2
  155.1 39.9 reduce-scatter.8
  197.5 48.1 reduce-scatter.10
  280.5 253.3 all-reduce.1
where the time goes:
time: 543 us; the launch traced here: 542 us
  waiting for transfers between devices  374 us (69%)
  blocking collectives  55.4 us (10%)
  local copies, waits for them, and re-layouts  37.9 us (7%)
  matrix products  29 us (5%)
  starting transfers between devices  22.8 us (4%)
  between operations  14 us (3%)
  other arithmetic  8.99 us (2%)
    psum x1, waiting for transfers between devices, per_device(): router_sum = lax.psum(router_term, ('expert', 'hidden'))  251 us
    unnamed x7, waiting for transfers between devices  71.7 us
    all_to_all x2, blocking collectives, to_experts(): lax.all_to_all(stacked_slots, 'expert', split_axis=2, concat_axis=0, tile...  55.4 us
    all_gather x2, waiting for transfers between devices, to_experts(): arrived = lax.all_gather(crossed, 'hidden', axis=0, tiled=True)  44.3 us
    all_to_all x2, starting transfers between devices, to_owners(): lax.all_to_all(summed, 'expert', split_axis=0, concat_axis=2, tiled=True)  22 us
    unnamed x29, local copies, waits for them, and re-layouts  15.3 us
  transfers between devices with their start and end apart: 7, of which 6 were waited for; matrix products, arithmetic and copies ran while one was open for 7% of the time, Pallas kernels for 0%

commit v1 on v0

--- a/solution.py
+++ b/solution.py
@@ -6,6 +6,14 @@
 D = 768
 SLOTS = 2
 TOK = 196
+
+
+def _use_tables(inp):
+    piece_now = lax.axis_size("expert")
+    clean = jnp.split(inp, piece_now, axis=2)
+    t1 = jnp.stack(clean, axis=0)
+    back = lax.all_to_all(t1, concat_axis=0, axis_name="expert", split_axis=0)
+    return jnp.concatenate(back, axis=0)
 
 
 def gelu_value(values):
@@ -20,7 +28,7 @@
 
 
 def to_experts(stacked_slots):
-    crossed = lax.all_to_all(stacked_slots, "expert", split_axis=2, concat_axis=0, tiled=True)
+    crossed = _use_tables(stacked_slots)
     arrived = lax.all_gather(crossed, "hidden", axis=0, tiled=True)
     return arrived
 

time: 543 us -> 568 us (1.046)
  blocking collectives: 55.4 us -> 26.2 us
  local copies, waits for them, and re-layouts: 37.9 us -> 64.3 us
  waiting for transfers between devices: 374 us -> 396 us
  starting transfers between devices: 22.8 us -> 37 us
  other arithmetic: 8.99 us -> 1.29 us
    unnamed x29 -> x154, local copies, waits for them, and re-layouts: 15.3 us -> 51.1 us
    all_to_all x2 -> x1, blocking collectives: 55.4 us -> 26.2 us  [_use_tables(): back = lax.all_to_all(t1, concat_axis=0, axis_name='expert', split_axis=0)]
    all_to_all x0 -> x1, starting transfers between devices: none -> 14.6 us  [_use_tables(): back = lax.all_to_all(t1, concat_axis=0, axis_name='expert', split_axis=0)]
    all_to_all x0 -> x1, waiting for transfers between devices: none -> 12.7 us  [_use_tables(): back = lax.all_to_all(t1, concat_axis=0, axis_name='expert', split_axis=0)]
    all_gather x2, waiting for transfers between devices: 44.3 us -> 55.2 us  [to_experts(): arrived = lax.all_gather(crossed, 'hidden', axis=0, tiled=True)]
    all_to_all x4 -> x0, local copies, waits for them, and re-layouts: 9.7 us -> none  [to_experts(): lax.all_to_all(stacked_slots, 'expert', split_axis=2, concat_axis=0, tile...]
    unnamed x2 -> x0, other arithmetic: 7.7 us -> none
  transfers between devices with their start and end apart: 7 -> 8, of which waited for: 6 -> 7; matrix products, arithmetic and copies ran while one was open for 7% -> 6% of each run, Pallas kernels for 0% -> 0%
where the time goes in v1:
time: 568 us; the launch traced here: 567 us
  waiting for transfers between devices  396 us (70%)
  local copies, waits for them, and re-layouts  64.3 us (11%)
  starting transfers between devices  37 us (7%)
  matrix products  28 us (5%)
  blocking collectives  26.2 us (5%)
  between operations  14.3 us (3%)
    psum x1, waiting for transfers between devices, per_device(): router_sum = lax.psum(router_term, ('expert', 'hidden'))  251 us
    unnamed x7, waiting for transfers between devices  71.5 us
    all_gather x2, waiting for transfers between devices, to_experts(): arrived = lax.all_gather(crossed, 'hidden', axis=0, tiled=True)  55.2 us
    unnamed x154, local copies, waits for them, and re-layouts  51.1 us
    all_to_all x1, blocking collectives, _use_tables(): back = lax.all_to_all(t1, concat_axis=0, axis_name='expert', split_axis=0)  26.2 us
    all_to_all x2, starting transfers between devices, to_owners(): lax.all_to_all(summed, 'expert', split_axis=0, concat_axis=2, tiled=True)  22 us
    all_to_all x1, starting transfers between devices, _use_tables(): back = lax.all_to_all(t1, concat_axis=0, axis_name='expert', split_axis=0)  14.6 us
    all_to_all x1, waiting for transfers between devices, _use_tables(): back = lax.all_to_all(t1, concat_axis=0, axis_name='expert', split_axis=0)  12.7 us
  transfers between devices with their start and end apart: 8, of which 7 were waited for; matrix products, arithmetic and copies ran while one was open for 6% of the time, Pallas kernels for 0%

profile of v1, /device:TPU:2, one launch (start us, length us, event | category | flops | bytes accessed | tf_op | source)
XLA Modules:
  0.0 567.2 jit_solution(12447457285687064407)
XLA Ops:
  7.2 1.6 fusion.40
  48.6 14.6 %all-to-all-start.1 = ((bf16[64,1,1,4,768]{4,3,2,1,0:T(4,128)(2,1)}), bf16[64,1,1,4,768]{4,3,2,1,0:T(4,128)(2,1)S(1)}, u32[]{:S(2)}, u32[]{:S(2)}) async-start(bf16[64,1,1,4,768]{4,3,2,1,0:T(4,128)(2,1)} %constant_dynamic-update-slice_fusion.64), calls=%async_computation.1 | async-start | bytes 786432 | tf_op jit(solution)/shard_map/all_to_all | solution.py:15
  64.7 12.7 %all-to-all-done.1 = bf16[64,1,1,4,768]{4,3,2,1,0:T(4,128)(2,1)S(1)} async-done(((bf16[64,1,1,4,768]{4,3,2,1,0:T(4,128)(2,1)}), bf16[64,1,1,4,768]{4,3,2,1,0:T(4,128)(2,1)S(1)}, u32[]{:S(2)}, u32[]{:S(2)}) %all-to-all-start.1) | async-done | bytes 393248 | tf_op jit(solution)/shard_map/all_to_all | solution.py:15
  84.0 26.2 %all_to_all.28 = bf16[64,1,1,4,768]{4,3,2,1,0:T(4,128)(2,1)} all-to-all(bf16[64,1,1,4,768]{4,3,2,1,0:T(4,128)(2,1)S(1)} %constant_dynamic-update-slice_fusion), channel_id=1, replica_groups=mesh['expert'=64,'hidden'=4] {'expert'}, dimensions={0} | all-to-all | bytes 786432 | tf_op jit(solution)/shard_map/all_to_all | solution.py:15
  110.3 16.4 %all-gather.7.cloned.1.call-done = bf16[256,1,1,4,768]{4,3,2,1,0:T(4,128)(2,1)} async-done(((bf16[64,1,1,4,768]{4,3,2,1,0:T(4,128)(2,1)}), bf16[256,1,1,4,768]{4,3,2,1,0:T(4,128)(2,1)}) %all-gather.7.cloned.1.call-update) | async-done | bytes 1572880 | tf_op jit(solution)/shard_map/all_gather | solution.py:32
  126.7 1.6 copy.22
  128.3 3.1 fusion.9
  131.4 38.8 %all-gather.5.cloned.1.call-done = bf16[256,1,1,4,768]{4,3,2,1,0:T(4,128)(2,1)} async-done(((bf16[64,1,1,4,768]{4,3,2,1,0:T(4,128)(2,1)}), bf16[256,1,1,4,768]{4,3,2,1,0:T(4,128)(2,1)}) %all-gather.5.cloned.1.call-update) | async-done | bytes 1572880 | tf_op jit(solution)/shard_map/all_gather | solution.py:32
  170.2 1.8 copy.21
  172.4 3.8 fusion.5
  180.5 3.5 fusion.18
  186.7 33.7 %reduce-scatter.9.cloned.1.call-done = bf16[64,3072]{1,0:T(8,128)(2,1)} async-done(((bf16[256,3072]{1,0:T(8,128)(2,1)}), bf16[64,3072]{1,0:T(8,128)(2,1)}) %reduce-scatter.9.cloned.1.call-update) | async-done | bytes 393232
  220.4 2.0 reshape.158
  222.4 10.8 %all-to-all-start.2 = ((bf16[64,1,4,768]{3,2,1,0:T(4,128)(2,1)}), bf16[64,1,4,768]{3,2,1,0:T(4,128)(2,1)S(1)}, u32[]{:S(2)}, u32[]{:S(2)}) async-start(bf16[64,1,4,768]{3,2,1,0:T(4,128)(2,1)} %reshape.158), calls=%async_computation.2 | async-start | bytes 786432 | tf_op jit(solution)/shard_map/all_to_all | solution.py:41
  233.3 37.7 %reduce-scatter.11.cloned.1.call-done = bf16[64,3072]{1,0:T(8,128)(2,1)} async-done(((bf16[256,3072]{1,0:T(8,128)(2,1)}), bf16[64,3072]{1,0:T(8,128)(2,1)}) %reduce-scatter.11.cloned.1.call-update) | async-done | bytes 393232
  271.0 2.0 reshape.160
  273.0 11.1 %all-to-all-start.3 = ((bf16[64,1,4,768]{3,2,1,0:T(4,128)(2,1)}), bf16[64,1,4,768]{3,2,1,0:T(4,128)(2,1)}, u32[]{:S(2)}, u32[]{:S(2)}) async-start(bf16[64,1,4,768]{3,2,1,0:T(4,128)(2,1)} %reshape.160), calls=%async_computation.3 | async-start | bytes 786432 | tf_op jit(solution)/shard_map/all_to_all | solution.py:41
  284.2 4.8 bitcast_convert_fusion
  290.5 2.9 bitcast_convert_fusion.1
  294.8 5.3 all-to-all-done.3
  300.1 1.8 reshape.148
  301.9 1.5 multiply_reduce_fusion.1
  306.0 2.0 fusion.26
  308.0 251.3 %all-reduce.2.cloned.1.call-done = f32[768,256]{0,1:T(8,128)} async-done(((f32[768,256]{0,1:T(8,128)}), f32[768,256]{0,1:T(8,128)}) %all-reduce.2.cloned.1.call-update) | async-done | bytes 786448 | tf_op jit(solution)/shard_map/psum | solution.py:108
  (178 shorter events, 61.7 us)
Async XLA Ops:
  7.2 121.1 %copy-start = (bf16[2,768,768]{2,1,0:T(8,128)(2,1)S(1)}, bf16[2,768,768]{2,1,0:T(8,128)(2,1)}, u32[]{:S(2)}) copy-start(bf16[2,768,768]{2,1,0:T(8,128)(2,1)} %param.8) | copy-start | bytes 7077892
  7.2 56.1 %copy-start.9 = (bf16[196,768]{1,0:T(8,128)(2,1)S(1)}, bf16[196,768]{1,0:T(8,128)(2,1)}, u32[]{:S(2)}) copy-start(bf16[196,768]{1,0:T(8,128)(2,1)} %param.6) | copy-start | bytes 903172
  48.6 28.8 %all-to-all-start.1 = ((bf16[64,1,1,4,768]{4,3,2,1,0:T(4,128)(2,1)}), bf16[64,1,1,4,768]{4,3,2,1,0:T(4,128)(2,1)S(1)}, u32[]{:S(2)}, u32[]{:S(2)}) async-start(bf16[64,1,1,4,768]{4,3,2,1,0:T(4,128)(2,1)} %constant_dynamic-update-slice_fusion.64), calls=%async_computation.1 | async-start | bytes 786432 | tf_op jit(solution)/shard_map/all_to_all | solution.py:15
  63.2 63.5 %all-gather.7.cloned.1.call-start = ((), (), s32[]{:S(2)}) async-start(), calls=%async_computation.8 | async-start | bytes 1966080 | tf_op jit(solution)/shard_map/all_gather | solution.py:32
  63.7 0.9 copy-start.7
  77.4 0.7 copy-start.4
  78.2 92.0 %all-gather.5.cloned.1.call-start = ((), (), s32[]{:S(2)}) async-start(), calls=%async_computation.7 | async-start | bytes 1966080 | tf_op jit(solution)/shard_map/all_gather | solution.py:32
  110.3 110.2 %reduce-scatter.9.cloned.1.call-start = ((), (), s32[]{:S(2)}) async-start(), calls=%async_computation.9 | async-start | bytes 1966080
  170.2 2.1 copy-start.8
  172.0 4.1 copy-start.3
  176.1 1.4 copy-start.10
  180.3 90.7 %reduce-scatter.11.cloned.1.call-start = ((), (), s32[]{:S(2)}) async-start(), calls=%async_computation.10 | async-start | bytes 1966080
  222.4 50.6 %all-to-all-start.2 = ((bf16[64,1,4,768]{3,2,1,0:T(4,128)(2,1)}), bf16[64,1,4,768]{3,2,1,0:T(4,128)(2,1)S(1)}, u32[]{:S(2)}, u32[]{:S(2)}) async-start(bf16[64,1,4,768]{3,2,1,0:T(4,128)(2,1)} %reshape.158), calls=%async_computation.2 | async-start | bytes 786432 | tf_op jit(solution)/shard_map/all_to_all | solution.py:41
  273.0 16.0 %copy-start.5 = (bf16[64,1,4,768]{3,2,1,0:T(4,128)(2,1)}, bf16[64,1,4,768]{3,2,1,0:T(4,128)(2,1)S(1)}, u32[]{:S(2)}) copy-start(bf16[64,1,4,768]{3,2,1,0:T(4,128)(2,1)S(1)} %all-to-all-done.2) | copy-start | bytes 1179652
  273.0 27.1 %all-to-all-start.3 = ((bf16[64,1,4,768]{3,2,1,0:T(4,128)(2,1)}), bf16[64,1,4,768]{3,2,1,0:T(4,128)(2,1)}, u32[]{:S(2)}, u32[]{:S(2)}) async-start(bf16[64,1,4,768]{3,2,1,0:T(4,128)(2,1)} %reshape.160), calls=%async_computation.3 | async-start | bytes 786432 | tf_op jit(solution)/shard_map/all_to_all | solution.py:41
  284.2 275.1 %all-reduce.2.cloned.1.call-start = ((), (), s32[]{:S(2)}) async-start(), calls=%async_computation.6 | async-start | bytes 1572864 | tf_op jit(solution)/shard_map/psum | solution.py:108
  284.2 4.9 copy-start.1
  289.1 1.4 copy-start.11
  290.5 4.0 copy-start.2
  294.8 8.7 %copy-start.6 = (f32[196,256]{1,0:T(8,128)}, f32[196,256]{1,0:T(8,128)S(1)}, u32[]{:S(2)}) copy-start(f32[196,256]{1,0:T(8,128)S(1)} %convolution_bitcast_fusion.1) | copy-start | bytes 602116
Sparse Core Ops, SparseCore 0:
  78.3 48.3 all-gather.6
  128.5 41.6 all-gather.4
  180.4 39.9 reduce-scatter.8
  222.8 48.1 reduce-scatter.10
  305.9 253.3 all-reduce.1
